TPU v7x, 32 devices: a whole 2x2x4 slice. The times are simulated.
32 devices in a mesh: tiles: 16 (over z, y, x), depth: 2 (over core).
Axes of the slice: x: 2, y: 2, z: 4, core: 2. Of those that a mesh axis runs over, the one named last changes fastest.
Arguments:
- momentum: float32 [16, 16, 6300], P('tiles', 'depth'), may hold values from -6 to 6
- tracer: float32 [16, 16, 6300], P('tiles', 'depth'), may hold values from -6 to 6
- mom_diffusivity: float32 [16, 16, 6300], P('tiles', 'depth'), may hold values from 0.02 to 0.2
- tra_diffusivity: float32 [16, 16, 6300], P('tiles', 'depth'), may hold values from 0.02 to 0.2
- mixing: float32 [16, 16, 6300], P('tiles', 'depth'), may hold values from 0.05 to 0.4
- wet_mask: int32 [16, 6300], P('tiles'), may hold values 0 or 1
- neighbours: int32 [16, 4], P('tiles'), may hold values from -1 to 15, as said below
- source_edges: int32 [16, 4], P('tiles'), may hold values from 0 to 3, as said below
- flips: int32 [16, 4], P('tiles'), may hold values from 0 to 1
- mom_cotangent: float32 [16, 16, 6300], P('tiles', 'depth'), may hold values from -6 to 6
- tra_cotangent: float32 [16, 16, 6300], P('tiles', 'depth'), may hold values from -6 to 6
Outputs:
- final_momentum: float32 [16, 16, 6300], P('tiles', 'depth')
- final_tracer: float32 [16, 16, 6300], P('tiles', 'depth')
- grad_momentum: float32 [16, 16, 6300], P('tiles', 'depth')
- grad_tracer: float32 [16, 16, 6300], P('tiles', 'depth')
Inputs may be any that keep to these rules, and one draw needn't show every extreme that they name: `neighbours`: the neighbour relation is symmetric, also across the fold seam, where a tile's north edge faces another tile's north edge in reverse order; -1 marks a missing neighbour. `source_edges`: for north and south directions the facing edge is north or south, for east and west directions it is east or west.
All inputs are finite; a program needn't handle non-finite values. No bound on the sum of `wet_mask` on one device may be relied on, other than what follows from the above.
Results may differ from a plain program's by a relative error of at most 0.00002.
Values sent between devices are 32-bit elements; how exact they have to be, the bound alone decides.
A program may use at most 64 MiB of HBM per device.

v0:
```python
import jax
import jax.numpy as jnp
from jax import lax
from jax.sharding import PartitionSpec as P

NI = 90
NJ = 70


def padded_2(block, sides, width):
    for axis, dim in sides:
        count = lax.axis_size(axis)
        forward = [(i, i + 1) for i in range(count - 1)]
        backward = [(target, source) for source, target in forward]
        low = lax.ppermute(
            lax.slice_in_dim(block, block.shape[dim] - width, None, axis=dim), axis, forward
        )
        high = lax.ppermute(lax.slice_in_dim(block, 0, width, axis=dim), axis, backward)
        block = jnp.concatenate([low, block, high], axis=dim)
    return block


def carried_in(part, axis, combine, identity, reverse):
    count = lax.axis_size(axis)
    place = lax.axis_index(axis)
    ahead = count - 1 - place if reverse else place
    gathered = lax.all_gather(part, axis)
    state = jnp.zeros_like(part) + jnp.asarray(identity, part.dtype)

    def one(hop, state):
        source = count - 1 - hop if reverse else hop
        return combine(state, lax.dynamic_index_in_dim(gathered, source, 0, False))

    return lax.fori_loop(0, ahead, one, state)


def edges_of(field):
    total = field.shape[-1]
    return jnp.concatenate(
        [field[..., total - NI :], field[..., :NI], field[..., NI - 1 :: NI], field[..., ::NI]],
        axis=-1,
    )


def pick_edge(chosen, source, flip, direction):
    if direction < 2:
        strip = jnp.where(source[:, None, None] == 0, chosen[..., :NI], chosen[..., NI : 2 * NI])
    else:
        strip = jnp.where(
            source[:, None, None] == 2,
            chosen[..., 2 * NI : 2 * NI + NJ],
            chosen[..., 2 * NI + NJ :],
        )
    return jnp.where(flip[:, None, None] == 1, strip[..., ::-1], strip)


def select_strips(neighbours, source_edges, flips, carry, pieces):
    spans = [(0, NI), (NI, NI), (2 * NI, NJ), (2 * NI + NJ, NJ)]
    results = []
    for held, piece in zip(carry, pieces):
        count = piece.shape[0]
        strips = []
        for direction in range(4):
            target = neighbours[:, direction]
            valid = (target >= 0) & (target < count)
            row_index = jnp.clip(target, 0, count - 1)
            chosen = jnp.take(piece, row_index, axis=0)
            strip = pick_edge(chosen, source_edges[:, direction], flips[:, direction], direction)
            offset, length = spans[direction]
            strips.append(
                jnp.where(valid[:, None, None], strip, held[..., offset : offset + length])
            )
        results.append(jnp.concatenate(strips, axis=-1))
    return tuple(results)


def shifted_sum(values, halo):
    total = values.shape[-1]
    column = jnp.arange(total) % NI
    north = jnp.concatenate([values[..., NI:], halo[..., :NI]], axis=-1)
    south = jnp.concatenate([halo[..., NI : 2 * NI], values[..., : total - NI]], axis=-1)
    east_halo = jnp.repeat(halo[..., 2 * NI : 2 * NI + NJ], NI, axis=-1)
    west_halo = jnp.repeat(halo[..., 2 * NI + NJ :], NI, axis=-1)
    east = jnp.where(
        column == NI - 1, east_halo, jnp.concatenate([values[..., 1:], values[..., :1]], axis=-1)
    )
    west = jnp.where(
        column == 0, west_halo, jnp.concatenate([values[..., -1:], values[..., :-1]], axis=-1)
    )
    return north + south + east + west


def laplace(field, weighted_halo, wet, wet_halo):
    values = shifted_sum(wet * field, weighted_halo)
    weights = shifted_sum(wet, wet_halo)
    return wet * (values - weights * field)


def add_one(earlier, later):
    return earlier + later


def local(
    momentum,
    tracer,
    mom_diffusivity,
    tra_diffusivity,
    mixing,
    wet_mask,
    neighbours,
    source_edges,
    flips,
    mom_cotangent,
    tra_cotangent,
):
    slot_count = momentum.shape[0]
    level_count = momentum.shape[1]
    edge_cells = 2 * NI + 2 * NJ
    depth_count = lax.axis_size("depth")
    depth_index = lax.axis_index("depth")
    levels_all = level_count * depth_count
    press_scale = levels_all ** (-0.5)
    level_index = depth_index * level_count + jnp.arange(level_count)
    has_above = (level_index > 0).astype(jnp.float32)[None, :, None]
    has_below = (level_index < levels_all - 1).astype(jnp.float32)[None, :, None]

    def fold_strips(carry, pieces):
        return select_strips(neighbours, source_edges, flips, carry, pieces)

    mask_start = jnp.zeros((slot_count, 1, edge_cells), jnp.int32)
    wet_halo = fold_strips(
        (mask_start,),
        (lax.all_gather(edges_of(wet_mask[:, None, :]), "tiles", axis=0, tiled=True),),
    )[0]
    wet_halo = wet_halo.astype(jnp.float32)
    wet = wet_mask[:, None, :].astype(jnp.float32)
    zeros_edge = jnp.zeros((slot_count, level_count, edge_cells), jnp.float32)
    zeros_cells = jnp.zeros((slot_count, momentum.shape[2]), jnp.float32)

    def vertical_from(field, above, below):
        return has_above * (above - field) + has_below * (below - field)

    def level_halo(field):
        padded = padded_2(field, (("depth", 1),), 1)
        return (padded[:, :-2], padded[:, 2:])

    mom_now, tra_now = (momentum, tracer)
    for iteration in range(2):
        own_sum = jnp.cumsum(tra_now, axis=1)
        above, below = level_halo(tra_now)
        prior_own = carried_in(own_sum[:, -1], "depth", add_one, zeros_cells, False)
        press = press_scale * (own_sum + prior_own[:, None, :])
        mom_halo, tra_halo, press_halo = fold_strips(
            (zeros_edge, zeros_edge, zeros_edge),
            (
                lax.all_gather(edges_of(mom_now), "tiles", axis=0, tiled=True),
                lax.all_gather(edges_of(tra_now), "tiles", axis=0, tiled=True),
                lax.all_gather(edges_of(press), "tiles", axis=0, tiled=True),
            ),
        )
        mom_next = (
            mom_now
            + mom_diffusivity * laplace(mom_now, wet_halo * mom_halo, wet, wet_halo)
            - 0.1 * laplace(press, wet_halo * press_halo, wet, wet_halo)
        )
        tra_next = (
            tra_now
            + tra_diffusivity * laplace(tra_now, wet_halo * tra_halo, wet, wet_halo)
            + mixing * vertical_from(tra_now, above, below)
            + 0.2 * mom_now
        )
        mom_now, tra_now = (mom_next, tra_next)
    mom_adjoint, tra_adjoint = (mom_cotangent, tra_cotangent)
    for iteration in range(2):
        mom_weighted = mom_diffusivity * mom_adjoint
        tra_weighted = tra_diffusivity * tra_adjoint
        cycle_mom, cycle_plain, cycle_tra = fold_strips(
            (zeros_edge, zeros_edge, zeros_edge),
            (
                lax.all_gather(edges_of(wet * mom_weighted), "tiles", axis=0, tiled=True),
                lax.all_gather(edges_of(wet * mom_adjoint), "tiles", axis=0, tiled=True),
                lax.all_gather(edges_of(wet * tra_weighted), "tiles", axis=0, tiled=True),
            ),
        )
        press_adjoint = -0.1 * laplace(mom_adjoint, cycle_plain, wet, wet_halo)
        mixed = mixing * tra_adjoint
        later_sum = jnp.flip(jnp.cumsum(jnp.flip(press_adjoint, axis=1), axis=1), axis=1)
        after = carried_in(later_sum[:, 0], "depth", add_one, zeros_cells, True)
        above, below = level_halo(mixed)
        press_back = press_scale * (later_sum + after[:, None, :])
        mom_back = mom_adjoint + laplace(mom_weighted, cycle_mom, wet, wet_halo) + 0.2 * tra_adjoint
        tra_back = (
            tra_adjoint
            + laplace(tra_weighted, cycle_tra, wet, wet_halo)
            + vertical_from(mixed, above, below)
            + press_back
        )
        mom_adjoint, tra_adjoint = (mom_back, tra_back)
    return (mom_now, tra_now, mom_adjoint, tra_adjoint)


def solution(mesh):
    in_specs = (
        P("tiles", "depth", None),
        P("tiles", "depth", None),
        P("tiles", "depth", None),
        P("tiles", "depth", None),
        P("tiles", "depth", None),
        P("tiles", None),
        P("tiles", None),
        P("tiles", None),
        P("tiles", None),
        P("tiles", "depth", None),
        P("tiles", "depth", None),
    )
    out_specs = (
        P("tiles", "depth", None),
        P("tiles", "depth", None),
        P("tiles", "depth", None),
        P("tiles", "depth", None),
    )
    return jax.shard_map(local, mesh=mesh, in_specs=in_specs, out_specs=out_specs, check_vma=False)
```

profile of v0, /device:TPU:0, one launch (start us, length us, event | category | flops | bytes accessed | tf_op | source)
XLA Modules:
  0.0 668.3 jit_solution(13493256316628074655)
XLA Ops:
  19.5 42.5 %all_gather.51 = s32[16,1,320]{2,1,0:T(1,128)S(1)} all-gather(s32[1,1,320]{2,1,0:T(1,128)S(1)} %pad_add_fusion), channel_id=1, replica_groups=mesh['tiles'=16,'depth'=2] {'tiles'}, dimensions={0}, use_global_device_ids=true | all-gather | bytes 21760 | tf_op jit(solution)/shard_map/all_gather | solution.py:133
  65.6 36.5 %all_gather.60 = f32[16,8,320]{2,1,0:T(8,128)S(1)} all-gather(f32[1,8,320]{2,1,0:T(8,128)S(1)} %pad_maximum_fusion.14), channel_id=1, replica_groups=mesh['tiles'=16,'depth'=2] {'tiles'}, dimensions={0}, use_global_device_ids=true | all-gather | bytes 174080 | tf_op jit(solution)/shard_map/all_gather | solution.py:180
  103.1 38.7 %all_gather.56 = f32[16,8,320]{2,1,0:T(8,128)S(1)} all-gather(f32[1,8,320]{2,1,0:T(8,128)S(1)} %pad_maximum_fusion.11), channel_id=1, replica_groups=mesh['tiles'=16,'depth'=2] {'tiles'}, dimensions={0}, use_global_device_ids=true | all-gather | bytes 174080 | tf_op jit(solution)/shard_map/all_gather | solution.py:157
  144.7 2.0 broadcast_multiply_fusion.12
  148.3 1.9 collective-permute-start.4
  152.2 4.2 collective-permute-start
  167.8 36.6 %all_gather.66 = f32[16,8,320]{2,1,0:T(8,128)S(1)} all-gather(f32[1,8,320]{2,1,0:T(8,128)S(1)} %pad_maximum_fusion.19), channel_id=1, replica_groups=mesh['tiles'=16,'depth'=2] {'tiles'}, dimensions={0}, use_global_device_ids=true | all-gather | bytes 174080 | tf_op jit(solution)/shard_map/all_gather | solution.py:181
  212.8 38.4 %all_gather.52 = f32[16,8,320]{2,1,0:T(8,128)S(1)} all-gather(f32[1,8,320]{2,1,0:T(8,128)S(1)} %pad_maximum_fusion.8), channel_id=1, replica_groups=mesh['tiles'=16,'depth'=2] {'tiles'}, dimensions={0}, use_global_device_ids=true | all-gather | bytes 174080 | tf_op jit(solution)/shard_map/all_gather | solution.py:156
  259.5 36.6 %all_gather.62 = f32[16,8,320]{2,1,0:T(8,128)S(1)} all-gather(f32[1,8,320]{2,1,0:T(8,128)S(1)} %pad_maximum_fusion.16), channel_id=1, replica_groups=mesh['tiles'=16,'depth'=2] {'tiles'}, dimensions={0}, use_global_device_ids=true | all-gather | bytes 174080 | tf_op jit(solution)/shard_map/all_gather | solution.py:182
  297.8 38.4 %all_gather.63 = f32[16,8,320]{2,1,0:T(8,128)S(1)} all-gather(f32[1,8,320]{2,1,0:T(8,128)S(1)} %pad_maximum_fusion.17), channel_id=1, replica_groups=mesh['tiles'=16,'depth'=2] {'tiles'}, dimensions={0}, use_global_device_ids=true | all-gather | bytes 174080 | tf_op jit(solution)/shard_map/all_gather | solution.py:181
  342.2 1.8 all_gather.64
  345.0 36.6 %all_gather.61 = f32[16,8,320]{2,1,0:T(8,128)S(1)} all-gather(f32[1,8,320]{2,1,0:T(8,128)S(1)} %pad_maximum_fusion.15), channel_id=1, replica_groups=mesh['tiles'=16,'depth'=2] {'tiles'}, dimensions={0}, use_global_device_ids=true | all-gather | bytes 174080 | tf_op jit(solution)/shard_map/all_gather | solution.py:180
  385.6 1.8 all_gather.53
  389.1 14.9 %rev.214 = f32[1,8,6300]{2,1,0:T(8,128)} reverse(f32[1,8,6300]{2,1,0:T(8,128)S(1)} %reduce_window_sum.27), dimensions={1} | reverse | bytes 403200 | tf_op jit(solution)/shard_map/jit(_flip)/rev | solution.py:187
  423.3 1.8 all_gather.57
  429.4 38.4 %all_gather.59 = f32[16,8,320]{2,1,0:T(8,128)S(1)} all-gather(f32[1,8,320]{2,1,0:T(8,128)S(1)} %pad_maximum_fusion.13), channel_id=1, replica_groups=mesh['tiles'=16,'depth'=2] {'tiles'}, dimensions={0}, use_global_device_ids=true | all-gather | bytes 174080 | tf_op jit(solution)/shard_map/all_gather | solution.py:157
  468.8 36.7 %all_gather.54 = f32[16,8,320]{2,1,0:T(8,128)S(1)} all-gather(f32[1,8,320]{2,1,0:T(8,128)S(1)} %pad_maximum_fusion.9), channel_id=1, replica_groups=mesh['tiles'=16,'depth'=2] {'tiles'}, dimensions={0}, use_global_device_ids=true | all-gather | bytes 174080 | tf_op jit(solution)/shard_map/all_gather | solution.py:158
  506.5 38.4 %all_gather.58 = f32[16,8,320]{2,1,0:T(8,128)S(1)} all-gather(f32[1,8,320]{2,1,0:T(8,128)S(1)} %pad_maximum_fusion.12), channel_id=1, replica_groups=mesh['tiles'=16,'depth'=2] {'tiles'}, dimensions={0}, use_global_device_ids=true | all-gather | bytes 174080 | tf_op jit(solution)/shard_map/all_gather | solution.py:158
  556.4 36.8 %all_gather.65 = f32[16,8,320]{2,1,0:T(8,128)S(1)} all-gather(f32[1,8,320]{2,1,0:T(8,128)S(1)} %pad_maximum_fusion.18), channel_id=1, replica_groups=mesh['tiles'=16,'depth'=2] {'tiles'}, dimensions={0}, use_global_device_ids=true | all-gather | bytes 174080 | tf_op jit(solution)/shard_map/all_gather | solution.py:182
  595.2 1.9 collective-permute-start.2
  601.0 4.2 collective-permute-start.6
  615.0 3.4 fusion.19
  619.9 38.2 %all_gather.55 = f32[16,8,320]{2,1,0:T(8,128)S(1)} all-gather(f32[1,8,320]{2,1,0:T(8,128)S(1)} %pad_maximum_fusion.10), channel_id=1, replica_groups=mesh['tiles'=16,'depth'=2] {'tiles'}, dimensions={0}, use_global_device_ids=true | all-gather | bytes 174080 | tf_op jit(solution)/shard_map/all_gather | solution.py:156
  663.1 2.7 fusion.48
  (577 shorter events, 120.1 us)
Async XLA Ops:
  1.4 7.8 %copy-start.3 = (f32[1,8,6300]{2,1,0:T(8,128)S(1)}, f32[1,8,6300]{2,1,0:T(8,128)}, u32[]{:S(2)}) copy-start(f32[1,8,6300]{2,1,0:T(8,128)} %param.24) | copy-start | bytes 604804
  6.6 5.6 copy-start.23
  102.7 43.9 %copy-start.6 = (f32[1,8,6300]{2,1,0:T(8,128)S(1)}, f32[1,8,6300]{2,1,0:T(8,128)}, u32[]{:S(2)}) copy-start(f32[1,8,6300]{2,1,0:T(8,128)} %param.33) | copy-start | bytes 604804
  103.1 43.5 %copy-start.5 = (f32[1,8,6300]{2,1,0:T(8,128)S(1)}, f32[1,8,6300]{2,1,0:T(8,128)}, u32[]{:S(2)}) copy-start(f32[1,8,6300]{2,1,0:T(8,128)} %param.32) | copy-start | bytes 604804
  142.4 4.2 copy-start.2
  143.1 3.6 copy-start.1
  143.2 3.5 copy-start
  148.3 263.5 %collective-permute-start.4 = (f32[1,1,6300]{2,1,0:T(1,128)}, f32[1,1,6300]{2,1,0:T(1,128)}, u32[]{:S(2)}, u32[]{:S(2)}) collective-permute-start(f32[1,1,6300]{2,1,0:T(1,128)} %get-tuple-element.272), channel_id=1, source_target_pairs={{0,1},{2,3},{4,5},{6,7},{8,9},{10,11},{12,13},{14,15},{16,17},{18,... | collective-permute-start | bytes 75608 | tf_op jit(solution)/shard_map/ppermute | solution.py:15
  150.2 261.7 %collective-permute-start.5 = (f32[1,1,6300]{2,1,0:T(1,128)}, f32[1,1,6300]{2,1,0:T(1,128)}, u32[]{:S(2)}, u32[]{:S(2)}) collective-permute-start(f32[1,1,6300]{2,1,0:T(1,128)} %get-tuple-element.273), channel_id=1, source_target_pairs={{1,0},{3,2},{5,4},{7,6},{9,8},{11,10},{13,12},{15,14},{17,16},{19,... | collective-permute-start | bytes 75608 | tf_op jit(solution)/shard_map/ppermute | solution.py:18
  152.2 268.4 %collective-permute-start = (f32[1,1,6300]{2,1,0:T(1,128)}, f32[1,1,6300]{2,1,0:T(1,128)}, u32[]{:S(2)}, u32[]{:S(2)}) collective-permute-start(f32[1,1,6300]{2,1,0:T(1,128)} %get-tuple-element.349), channel_id=1, source_target_pairs={{0,1},{2,3},{4,5},{6,7},{8,9},{10,11},{12,13},{14,15},{16,17},{18,... | collective-permute-start | bytes 75608 | tf_op jit(solution)/shard_map/ppermute | solution.py:15
  156.4 264.2 %collective-permute-start.1 = (f32[1,1,6300]{2,1,0:T(1,128)}, f32[1,1,6300]{2,1,0:T(1,128)}, u32[]{:S(2)}, u32[]{:S(2)}) collective-permute-start(f32[1,1,6300]{2,1,0:T(1,128)} %get-tuple-element.350), channel_id=1, source_target_pairs={{1,0},{3,2},{5,4},{7,6},{9,8},{11,10},{13,12},{15,14},{17,16},{19,... | collective-permute-start | bytes 75608 | tf_op jit(solution)/shard_map/ppermute | solution.py:18
  251.2 3.1 copy-start.95
  389.1 22.8 %copy-start.77 = (f32[8]{0:T(128)}, f32[8]{0:T(128)S(1)}, u32[]{:S(2)}) copy-start(f32[8]{0:T(128)S(1)} %get-tuple-element.455) | copy-start | bytes 100
  389.1 22.8 %copy-start.81 = (f32[8]{0:T(128)}, f32[8]{0:T(128)S(1)}, u32[]{:S(2)}) copy-start(f32[8]{0:T(128)S(1)} %get-tuple-element.456) | copy-start | bytes 100
  417.6 3.0 copy-start.9
  595.2 19.0 %collective-permute-start.2 = (f32[1,1,6300]{2,1,0:T(1,128)}, f32[1,1,6300]{2,1,0:T(1,128)}, u32[]{:S(2)}, u32[]{:S(2)}) collective-permute-start(f32[1,1,6300]{2,1,0:T(1,128)} %get-tuple-element.339), channel_id=1, source_target_pairs={{0,1},{2,3},{4,5},{6,7},{8,9},{10,11},{12,13},{14,15},{16,17},{18,... | collective-permute-start | bytes 75608 | tf_op jit(solution)/shard_map/ppermute | solution.py:15
  597.1 17.2 %collective-permute-start.3 = (f32[1,1,6300]{2,1,0:T(1,128)}, f32[1,1,6300]{2,1,0:T(1,128)}, u32[]{:S(2)}, u32[]{:S(2)}) collective-permute-start(f32[1,1,6300]{2,1,0:T(1,128)} %get-tuple-element.340), channel_id=1, source_target_pairs={{1,0},{3,2},{5,4},{7,6},{9,8},{11,10},{13,12},{15,14},{17,16},{19,... | collective-permute-start | bytes 75608 | tf_op jit(solution)/shard_map/ppermute | solution.py:18
  601.0 64.8 %collective-permute-start.6 = (f32[1,1,6300]{2,1,0:T(1,128)}, f32[1,1,6300]{2,1,0:T(1,128)}, u32[]{:S(2)}, u32[]{:S(2)}) collective-permute-start(f32[1,1,6300]{2,1,0:T(1,128)} %get-tuple-element.260), channel_id=1, source_target_pairs={{0,1},{2,3},{4,5},{6,7},{8,9},{10,11},{12,13},{14,15},{16,17},{18,... | collective-permute-start | bytes 75608 | tf_op jit(solution)/shard_map/ppermute | solution.py:15
  605.2 60.6 %collective-permute-start.7 = (f32[1,1,6300]{2,1,0:T(1,128)}, f32[1,1,6300]{2,1,0:T(1,128)}, u32[]{:S(2)}, u32[]{:S(2)}) collective-permute-start(f32[1,1,6300]{2,1,0:T(1,128)} %get-tuple-element.261), channel_id=1, source_target_pairs={{1,0},{3,2},{5,4},{7,6},{9,8},{11,10},{13,12},{15,14},{17,16},{19,... | collective-permute-start | bytes 75608 | tf_op jit(solution)/shard_map/ppermute | solution.py:18
  663.1 2.8 copy-start.8
  663.1 2.8 copy-start.14
  663.1 2.8 copy-start.15
  663.1 2.8 copy-start.21
  663.1 2.8 copy-start.36
  (80 other events, 65.1 us)
where the time goes:
time: 670 us; the launch traced here: 668 us
  blocking collectives  500 us (75%)
  local copies, waits for them, and re-layouts  98.7 us (15%)
  other arithmetic  37 us (6%)
  starting transfers between devices  17.3 us (3%)
  between operations  15 us (2%)
    all_gather x2, blocking collectives, local(): lax.all_gather(edges_of(tra_now), 'tiles', axis=0, tiled=True)  77.1 us
    all_gather x2, blocking collectives, local(): lax.all_gather(edges_of(mom_now), 'tiles', axis=0, tiled=True)  76.6 us
    all_gather x2, blocking collectives, local(): lax.all_gather(edges_of(press), 'tiles', axis=0, tiled=True)  75 us
    all_gather x2, blocking collectives, local(): lax.all_gather(edges_of(wet * mom_adjoint), 'tiles', axis=0, tiled=True)  75 us
    all_gather x2, blocking collectives, local(): lax.all_gather(edges_of(wet * tra_weighted), 'tiles', axis=0, tiled=True)  73.4 us
    all_gather x2, blocking collectives, local(): lax.all_gather(edges_of(wet * mom_weighted), 'tiles', axis=0, tiled=True)  73.1 us
    all_gather x1, blocking collectives, local(): lax.all_gather(edges_of(wet_mask[:, None, :]), 'tiles', axis=0, tiled=True)  42.5 us
    rev x2, local copies, waits for them, and re-layouts, local(): jnp.flip(jnp.cumsum(jnp.flip(press_adjoint, axis=1), axis=1), axis=1)  15.6 us
  transfers between devices with their start and end apart: 8, of which 0 were waited for; matrix products, arithmetic and copies ran while one was open for 13% of the time, Pallas kernels for 0%

commit v1 on v0

--- a/solution.py
+++ b/solution.py
@@ -5,6 +5,18 @@
 
 NI = 90
 NJ = 70
+
+
+def doubled_up(array, axis, dim):
+    ways, here, step = (lax.axis_size(axis), lax.axis_index(axis), array.shape[dim])
+    line, have = (array, 1)
+    while have < ways:
+        line = jnp.concatenate(
+            [line, lax.ppermute(line, axis, [(d, (d - have) % ways) for d in range(ways)])],
+            axis=dim,
+        )
+        have = 2 * have
+    return jnp.roll(line, here * step, axis=dim)
 
 
 def padded_2(block, sides, width):
@@ -153,7 +165,7 @@
         mom_halo, tra_halo, press_halo = fold_strips(
             (zeros_edge, zeros_edge, zeros_edge),
             (
-                lax.all_gather(edges_of(mom_now), "tiles", axis=0, tiled=True),
+                doubled_up(edges_of(mom_now), "tiles", 0),
                 lax.all_gather(edges_of(tra_now), "tiles", axis=0, tiled=True),
                 lax.all_gather(edges_of(press), "tiles", axis=0, tiled=True),
             ),

time: 670 us -> 627 us (0.936)
  blocking collectives: 500 us -> 426 us
  waiting for transfers between devices: 0.02 us -> 24.1 us
    all_gather x2 -> x0, blocking collectives: 76.6 us -> none  [local(): lax.all_gather(edges_of(mom_now), 'tiles', axis=0, tiled=True)]
    ppermute x0 -> x8, waiting for transfers between devices: none -> 24 us  [doubled_up(): lax.ppermute(line, axis, [(d, (d - have) % ways) for d in range(ways)])]
    unnamed x192 -> x258, local copies, waits for them, and re-layouts: 12.2 us -> 17.1 us
  transfers between devices with their start and end apart: 8 -> 16, of which waited for: 0 -> 6; matrix products, arithmetic and copies ran while one was open for 13% -> 14% of each run, Pallas kernels for 0% -> 0%
where the time goes in v1:
time: 627 us; the launch traced here: 622 us
  blocking collectives  426 us (68%)
  local copies, waits for them, and re-layouts  96.7 us (15%)
  other arithmetic  43.3 us (7%)
  waiting for transfers between devices  24.1 us (4%)
  starting transfers between devices  16.3 us (3%)
  between operations  15.6 us (2%)
    all_gather x2, blocking collectives, local(): lax.all_gather(edges_of(wet * mom_adjoint), 'tiles', axis=0, tiled=True)  76.4 us
    all_gather x2, blocking collectives, local(): lax.all_gather(edges_of(wet * tra_weighted), 'tiles', axis=0, tiled=True)  75.8 us
    all_gather x2, blocking collectives, local(): lax.all_gather(edges_of(tra_now), 'tiles', axis=0, tiled=True)  75.7 us
    all_gather x2, blocking collectives, local(): lax.all_gather(edges_of(press), 'tiles', axis=0, tiled=True)  75 us
    all_gather x2, blocking collectives, local(): lax.all_gather(edges_of(wet * mom_weighted), 'tiles', axis=0, tiled=True)  73.4 us
    all_gather x1, blocking collectives, local(): lax.all_gather(edges_of(wet_mask[:, None, :]), 'tiles', axis=0, tiled=True)  42.5 us
    ppermute x8, waiting for transfers between devices, doubled_up(): lax.ppermute(line, axis, [(d, (d - have) % ways) for d in range(ways)])  24 us
    unnamed x258, local copies, waits for them, and re-layouts  17.1 us
  transfers between devices with their start and end apart: 16, of which 6 were waited for; matrix products, arithmetic and copies ran while one was open for 14% of the time, Pallas kernels for 0%

profile of v1, /device:TPU:0, one launch (start us, length us, event | category | flops | bytes accessed | tf_op | source)
XLA Modules:
  0.0 622.0 jit_solution(2764073047667400929)
XLA Ops:
  19.7 42.5 %all_gather.45 = s32[16,1,320]{2,1,0:T(1,128)S(1)} all-gather(s32[1,1,320]{2,1,0:T(1,128)S(1)} %pad_add_fusion), channel_id=1, replica_groups=mesh['tiles'=16,'depth'=2] {'tiles'}, dimensions={0}, use_global_device_ids=true | all-gather | bytes 21760 | tf_op jit(solution)/shard_map/all_gather | solution.py:145
  66.4 36.5 %all_gather.52 = f32[16,8,320]{2,1,0:T(8,128)S(1)} all-gather(f32[1,8,320]{2,1,0:T(8,128)S(1)} %pad_maximum_fusion.20), channel_id=1, replica_groups=mesh['tiles'=16,'depth'=2] {'tiles'}, dimensions={0}, use_global_device_ids=true | all-gather | bytes 174080 | tf_op jit(solution)/shard_map/all_gather | solution.py:192
  104.0 38.7 %all_gather.48 = f32[16,8,320]{2,1,0:T(8,128)S(1)} all-gather(f32[1,8,320]{2,1,0:T(8,128)S(1)} %pad_maximum_fusion.17), channel_id=1, replica_groups=mesh['tiles'=16,'depth'=2] {'tiles'}, dimensions={0}, use_global_device_ids=true | all-gather | bytes 174080 | tf_op jit(solution)/shard_map/all_gather | solution.py:169
  145.5 2.0 broadcast_multiply_fusion.12
  149.5 1.9 collective-permute-start.12
  154.8 4.2 collective-permute-start.8
  170.5 38.3 %all_gather.58 = f32[16,8,320]{2,1,0:T(8,128)S(1)} all-gather(f32[1,8,320]{2,1,0:T(8,128)S(1)} %pad_maximum_fusion.25), channel_id=1, replica_groups=mesh['tiles'=16,'depth'=2] {'tiles'}, dimensions={0}, use_global_device_ids=true | all-gather | bytes 174080 | tf_op jit(solution)/shard_map/all_gather | solution.py:193
  220.3 37.0 %all_gather.54 = f32[16,8,320]{2,1,0:T(8,128)S(1)} all-gather(f32[1,8,320]{2,1,0:T(8,128)S(1)} %pad_maximum_fusion.22), channel_id=1, replica_groups=mesh['tiles'=16,'depth'=2] {'tiles'}, dimensions={0}, use_global_device_ids=true | all-gather | bytes 174080 | tf_op jit(solution)/shard_map/all_gather | solution.py:194
  260.6 38.1 %all_gather.55 = f32[16,8,320]{2,1,0:T(8,128)S(1)} all-gather(f32[1,8,320]{2,1,0:T(8,128)S(1)} %pad_maximum_fusion.23), channel_id=1, replica_groups=mesh['tiles'=16,'depth'=2] {'tiles'}, dimensions={0}, use_global_device_ids=true | all-gather | bytes 174080 | tf_op jit(solution)/shard_map/all_gather | solution.py:193
  307.5 36.9 %all_gather.53 = f32[16,8,320]{2,1,0:T(8,128)S(1)} all-gather(f32[1,8,320]{2,1,0:T(8,128)S(1)} %pad_maximum_fusion.21), channel_id=1, replica_groups=mesh['tiles'=16,'depth'=2] {'tiles'}, dimensions={0}, use_global_device_ids=true | all-gather | bytes 174080 | tf_op jit(solution)/shard_map/all_gather | solution.py:192
  348.7 1.8 all_gather.59
  352.8 1.8 all_gather.46
  356.6 14.8 %rev.214 = f32[1,8,6300]{2,1,0:T(8,128)} reverse(f32[1,8,6300]{2,1,0:T(8,128)S(1)} %reduce_window_sum.27), dimensions={1} | reverse | bytes 403200 | tf_op jit(solution)/shard_map/jit(_flip)/rev | solution.py:199
  393.0 38.8 %all_gather.57 = f32[16,8,320]{2,1,0:T(8,128)S(1)} all-gather(f32[1,8,320]{2,1,0:T(8,128)S(1)} %pad_maximum_fusion.24), channel_id=1, replica_groups=mesh['tiles'=16,'depth'=2] {'tiles'}, dimensions={0}, use_global_device_ids=true | all-gather | bytes 174080 | tf_op jit(solution)/shard_map/all_gather | solution.py:194
  439.6 2.0 fusion.4
  442.9 8.5 %collective-permute-done.3 = f32[8,8,320]{2,1,0:T(8,128)S(1)} collective-permute-done((f32[8,8,320]{2,1,0:T(8,128)S(1)}, f32[8,8,320]{2,1,0:T(8,128)S(1)}, u32[]{:S(2)}, u32[]{:S(2)}) %collective-permute-start.3) | collective-permute-done | bytes 81952 | tf_op jit(solution)/shard_map/ppermute | solution.py:15
  461.2 36.9 %all_gather.51 = f32[16,8,320]{2,1,0:T(8,128)S(1)} all-gather(f32[1,8,320]{2,1,0:T(8,128)S(1)} %pad_maximum_fusion.19), channel_id=1, replica_groups=mesh['tiles'=16,'depth'=2] {'tiles'}, dimensions={0}, use_global_device_ids=true | all-gather | bytes 174080 | tf_op jit(solution)/shard_map/all_gather | solution.py:169
  499.1 38.0 %all_gather.47 = f32[16,8,320]{2,1,0:T(8,128)S(1)} all-gather(f32[1,8,320]{2,1,0:T(8,128)S(1)} %pad_maximum_fusion.15), channel_id=1, replica_groups=mesh['tiles'=16,'depth'=2] {'tiles'}, dimensions={0}, use_global_device_ids=true | all-gather | bytes 174080 | tf_op jit(solution)/shard_map/all_gather | solution.py:170
  538.2 37.0 %all_gather.50 = f32[16,8,320]{2,1,0:T(8,128)S(1)} all-gather(f32[1,8,320]{2,1,0:T(8,128)S(1)} %pad_maximum_fusion.18), channel_id=1, replica_groups=mesh['tiles'=16,'depth'=2] {'tiles'}, dimensions={0}, use_global_device_ids=true | all-gather | bytes 174080 | tf_op jit(solution)/shard_map/all_gather | solution.py:170
  584.8 1.9 collective-permute-start.10
  596.0 3.2 fusion.19
  603.9 3.7 collective-permute-done.5
  607.7 4.1 collective-permute-done.6
  611.9 5.9 collective-permute-done.7
  (665 shorter events, 132.0 us)
Async XLA Ops:
  1.4 7.8 %copy-start.3 = (f32[1,8,6300]{2,1,0:T(8,128)S(1)}, f32[1,8,6300]{2,1,0:T(8,128)}, u32[]{:S(2)}) copy-start(f32[1,8,6300]{2,1,0:T(8,128)} %param.26) | copy-start | bytes 604804
  6.7 5.6 copy-start.31
  103.6 43.9 %copy-start.6 = (f32[1,8,6300]{2,1,0:T(8,128)S(1)}, f32[1,8,6300]{2,1,0:T(8,128)}, u32[]{:S(2)}) copy-start(f32[1,8,6300]{2,1,0:T(8,128)} %param.35) | copy-start | bytes 604804
  104.0 43.5 %copy-start.5 = (f32[1,8,6300]{2,1,0:T(8,128)S(1)}, f32[1,8,6300]{2,1,0:T(8,128)}, u32[]{:S(2)}) copy-start(f32[1,8,6300]{2,1,0:T(8,128)} %param.34) | copy-start | bytes 604804
  147.5 5.2 copy-start.4
  149.5 233.4 %collective-permute-start.12 = (f32[1,1,6300]{2,1,0:T(1,128)}, f32[1,1,6300]{2,1,0:T(1,128)}, u32[]{:S(2)}, u32[]{:S(2)}) collective-permute-start(f32[1,1,6300]{2,1,0:T(1,128)} %get-tuple-element.277), channel_id=1, source_target_pairs={{0,1},{2,3},{4,5},{6,7},{8,9},{10,11},{12,13},{14,15},{16,17},{18,... | collective-permute-start | bytes 75608 | tf_op jit(solution)/shard_map/ppermute | solution.py:27
  151.4 231.5 %collective-permute-start.13 = (f32[1,1,6300]{2,1,0:T(1,128)}, f32[1,1,6300]{2,1,0:T(1,128)}, u32[]{:S(2)}, u32[]{:S(2)}) collective-permute-start(f32[1,1,6300]{2,1,0:T(1,128)} %get-tuple-element.278), channel_id=1, source_target_pairs={{1,0},{3,2},{5,4},{7,6},{9,8},{11,10},{13,12},{15,14},{17,16},{19,... | collective-permute-start | bytes 75608 | tf_op jit(solution)/shard_map/ppermute | solution.py:30
  154.2 225.9 %collective-permute-start = (f32[1,8,320]{2,1,0:T(8,128)}, f32[1,8,320]{2,1,0:T(8,128)}, u32[]{:S(2)}, u32[]{:S(2)}) collective-permute-start(f32[1,8,320]{2,1,0:T(8,128)} %get-tuple-element.240), channel_id=1, source_target_pairs={{0,30},{2,0},{4,2},{6,4},{8,6},{10,8},{12,10},{14,12},{16,14},{18,... | collective-permute-start | bytes 30728 | tf_op jit(solution)/shard_map/ppermute | solution.py:15
  154.8 299.8 %collective-permute-start.8 = (f32[1,1,6300]{2,1,0:T(1,128)}, f32[1,1,6300]{2,1,0:T(1,128)}, u32[]{:S(2)}, u32[]{:S(2)}) collective-permute-start(f32[1,1,6300]{2,1,0:T(1,128)} %get-tuple-element.354), channel_id=1, source_target_pairs={{0,1},{2,3},{4,5},{6,7},{8,9},{10,11},{12,13},{14,15},{16,17},{18,... | collective-permute-start | bytes 75608 | tf_op jit(solution)/shard_map/ppermute | solution.py:27
  159.0 295.6 %collective-permute-start.9 = (f32[1,1,6300]{2,1,0:T(1,128)}, f32[1,1,6300]{2,1,0:T(1,128)}, u32[]{:S(2)}, u32[]{:S(2)}) collective-permute-start(f32[1,1,6300]{2,1,0:T(1,128)} %get-tuple-element.355), channel_id=1, source_target_pairs={{1,0},{3,2},{5,4},{7,6},{9,8},{11,10},{13,12},{15,14},{17,16},{19,... | collective-permute-start | bytes 75608 | tf_op jit(solution)/shard_map/ppermute | solution.py:30
  376.8 6.1 copy-start.7
  381.5 55.1 %collective-permute-start.1 = (f32[2,8,320]{2,1,0:T(8,128)}, f32[2,8,320]{2,1,0:T(8,128)}, u32[]{:S(2)}, u32[]{:S(2)}) collective-permute-start(f32[2,8,320]{2,1,0:T(8,128)} %pad_maximum_fusion.12), channel_id=1, source_target_pairs={{0,28},{2,30},{4,0},{6,2},{8,4},{10,6},{12,8},{14,10},{16,12},{18,... | collective-permute-start | bytes 61448 | tf_op jit(solution)/shard_map/ppermute | solution.py:15
  433.8 5.2 copy-start.8
  433.8 5.2 copy-start.9
  433.9 5.0 collective-permute-start.14
  435.4 3.5 collective-permute-start.15
  437.5 4.5 collective-permute-start.2
  442.8 8.5 %collective-permute-start.3 = (f32[8,8,320]{2,1,0:T(8,128)S(1)}, f32[8,8,320]{2,1,0:T(8,128)S(1)}, u32[]{:S(2)}, u32[]{:S(2)}) collective-permute-start(f32[8,8,320]{2,1,0:T(8,128)S(1)} %pad_maximum_fusion.8), channel_id=1, source_target_pairs={{0,16},{2,18},{4,20},{6,22},{8,24},{10,26},{12,28},{14,30},{16,0},... | collective-permute-start | bytes 245768 | tf_op jit(solution)/shard_map/ppermute | solution.py:15
  584.8 10.4 %collective-permute-start.10 = (f32[1,1,6300]{2,1,0:T(1,128)}, f32[1,1,6300]{2,1,0:T(1,128)}, u32[]{:S(2)}, u32[]{:S(2)}) collective-permute-start(f32[1,1,6300]{2,1,0:T(1,128)} %get-tuple-element.344), channel_id=1, source_target_pairs={{0,1},{2,3},{4,5},{6,7},{8,9},{10,11},{12,13},{14,15},{16,17},{18,... | collective-permute-start | bytes 75608 | tf_op jit(solution)/shard_map/ppermute | solution.py:27
  586.7 8.5 %collective-permute-start.11 = (f32[1,1,6300]{2,1,0:T(1,128)}, f32[1,1,6300]{2,1,0:T(1,128)}, u32[]{:S(2)}, u32[]{:S(2)}) collective-permute-start(f32[1,1,6300]{2,1,0:T(1,128)} %get-tuple-element.345), channel_id=1, source_target_pairs={{1,0},{3,2},{5,4},{7,6},{9,8},{11,10},{13,12},{15,14},{17,16},{19,... | collective-permute-start | bytes 75608 | tf_op jit(solution)/shard_map/ppermute | solution.py:30
  600.0 3.7 collective-permute-start.4
  603.8 3.8 collective-permute-start.5
  607.7 4.1 collective-permute-start.6
  611.8 5.9 collective-permute-start.7
  (118 other events, 128.9 us)
